TPU v7x, 32 devices: a whole 2x2x4 slice. The times are simulated.
32 devices in a mesh: clip: 2 (over x), seq: 16 (over z, y, core).
Axes of the slice: x: 2, y: 2, z: 4, core: 2. Of those that a mesh axis runs over, the one named last changes fastest.
Arguments:
- video_query: bfloat16 [512, 4096], P(('clip', 'seq')), parts along dimension 0, may hold values from -6 to 6
- video_keys: bfloat16 [512, 4096], P(('clip', 'seq')), parts along dimension 0, may hold values from -6 to 6
- video_values: bfloat16 [512, 4096], P(('clip', 'seq')), parts along dimension 0, may hold values from -6 to 6
- audio_query: bfloat16 [256, 2048], P(('clip', 'seq')), parts along dimension 0, may hold values from -6 to 6
- audio_keys: bfloat16 [256, 2048], P(('clip', 'seq')), parts along dimension 0, may hold values from -6 to 6
- audio_values: bfloat16 [256, 2048], P(('clip', 'seq')), parts along dimension 0, may hold values from -6 to 6
- cross_video_query: bfloat16 [512, 2048], P(('clip', 'seq')), parts along dimension 0, may hold values from -6 to 6
- cross_video_keys: bfloat16 [512, 2048], P(('clip', 'seq')), parts along dimension 0, may hold values from -6 to 6
- cross_video_values: bfloat16 [512, 2048], P(('clip', 'seq')), parts along dimension 0, may hold values from -6 to 6
- cross_audio_query: bfloat16 [256, 2048], P(('clip', 'seq')), parts along dimension 0, may hold values from -6 to 6
- cross_audio_keys: bfloat16 [256, 2048], P(('clip', 'seq')), parts along dimension 0, may hold values from -6 to 6
- cross_audio_values: bfloat16 [256, 2048], P(('clip', 'seq')), parts along dimension 0, may hold values from -6 to 6
- video_length: int32 [2], P('clip'), parts along dimension 0, may hold values from 128 to 256
- audio_length: int32 [2], P('clip'), parts along dimension 0, may hold values from 64 to 128
- align_offset: int32 [2], P('clip'), parts along dimension 0, may hold values from -8 to 8
Outputs:
- video_mixed: bfloat16 [512, 4096], P(('clip', 'seq')), parts along dimension 0
- audio_mixed: bfloat16 [256, 2048], P(('clip', 'seq')), parts along dimension 0
- video_cross: bfloat16 [512, 2048], P(('clip', 'seq')), parts along dimension 0
- audio_cross: bfloat16 [256, 2048], P(('clip', 'seq')), parts along dimension 0
There are 2 independent parts, one for each index of `clip`. A program takes and returns all parts, laid end to end along the dimension named above; each array names one. Nothing has to cross between parts.
All inputs are finite; a program needn't handle non-finite values.
Results may differ from a plain program's by a relative error of at most 0.006.
Values may be sent and summed in bfloat16 or wider, within the bound.
A program may use at most 128 MiB of HBM per device.

v0:
```python
import math

import jax
import jax.numpy as jnp
from jax import lax
from jax.sharding import PartitionSpec as P

HV = 32
HDV = 128
HA = 32
HDA = 64


def block_size(total, limit):
    chosen = min(total, limit)
    while total % chosen:
        chosen -= 1
    return chosen


def split_heads(tokens, heads, depth, copies):
    rows = tokens.shape[0]
    shaped = tokens.reshape(copies, rows // copies, heads, depth).transpose(2, 0, 1, 3)
    return shaped.reshape(heads * copies, rows // copies, depth)


def spread_heads(tokens, heads, depth, copies):
    rows = tokens.shape[0]
    shaped = tokens.reshape(rows, heads, depth).transpose(1, 0, 2)
    shaped = jnp.broadcast_to(shaped[:, None], (heads, copies, rows, depth))
    return shaped.reshape(heads * copies, rows, depth)


def join_heads(owned, heads, depth, copies):
    part_rows = owned.shape[1]
    shaped = owned.reshape(heads, copies, part_rows, depth).transpose(1, 2, 0, 3)
    return shaped.reshape(copies * part_rows, heads * depth)


def owned_positions(rows, copies, devices, index):
    part_rows = rows // copies
    flat = jnp.arange(devices * part_rows, dtype=jnp.int32)
    return flat // part_rows * rows + index % copies * part_rows + flat % part_rows


def online_update(carry, scores, permit, value_tile, value_form):
    running, total, accum = carry
    scores = jnp.where(permit, scores, -1e30)
    newmax = jnp.maximum(running, jnp.max(scores, axis=2))
    weights = jnp.where(permit, jnp.exp(scores - newmax[:, :, None]), 0.0)
    factor = jnp.exp(running - newmax)
    total = total * factor + jnp.sum(weights, axis=2)
    mixed = jnp.einsum(
        value_form, weights.astype(jnp.bfloat16), value_tile, preferred_element_type=jnp.float32
    )
    accum = accum * factor[:, :, None] + mixed
    return (newmax, total, accum)


def fold_initial(rows, heads, depth):
    return (
        jnp.full((heads, rows), -1e30, jnp.float32),
        jnp.zeros((heads, rows), jnp.float32),
        jnp.zeros((heads, rows, depth), jnp.float32),
    )


def fold_piece(carry, local_query, key_rows, value_rows, permit, heads, depth):
    keyed = key_rows.reshape(key_rows.shape[0], heads, depth)
    valued = value_rows.reshape(value_rows.shape[0], heads, depth)
    scores = jnp.einsum("qhd,khd->hqk", local_query, keyed, preferred_element_type=jnp.float32) * (
        1.0 / math.sqrt(depth)
    )
    return online_update(carry, scores, permit[None], valued, "hqk,khd->hqd")


def fold_finish(carry, heads, depth):
    running, total, accum = carry
    result = (accum / total[:, :, None]).astype(jnp.bfloat16)
    return result.transpose(1, 0, 2).reshape(result.shape[1], heads * depth)


def attend_local(queries, keys, values, query_pos, key_pos, allowed):
    heads, q_count, depth = queries.shape
    k_count = keys.shape[1]
    q_block = block_size(q_count, 512)
    k_block = block_size(k_count, 2048)
    scale = 1.0 / math.sqrt(depth)
    q_tiles = queries.reshape(heads, q_count // q_block, q_block, depth).transpose(1, 0, 2, 3)
    k_tiles = keys.reshape(heads, k_count // k_block, k_block, depth).transpose(1, 0, 2, 3)
    v_tiles = values.reshape(heads, k_count // k_block, k_block, depth).transpose(1, 0, 2, 3)
    q_places = query_pos.reshape(q_count // q_block, q_block)
    k_places = key_pos.reshape(k_count // k_block, k_block)

    def one_tile(packed):
        q_tile, q_where = packed

        def absorb(carry, piece):
            k_tile, v_tile, k_where = piece
            scores = (
                jnp.einsum("hqd,hkd->hqk", q_tile, k_tile, preferred_element_type=jnp.float32)
                * scale
            )
            permit = allowed(q_where[:, None], k_where[None, :])[None]
            return (online_update(carry, scores, permit, v_tile, "hqk,hkd->hqd"), None)

        initial = fold_initial(q_block, heads, depth)
        final_state, unused = lax.scan(absorb, initial, (k_tiles, v_tiles, k_places))
        running, total, accum = final_state
        return (accum / total[:, :, None]).astype(jnp.bfloat16)

    tiles = lax.map(one_tile, (q_tiles, q_places))
    return tiles.transpose(1, 0, 2, 3).reshape(heads, q_count, depth)


def shards(
    video_query,
    video_keys,
    video_values,
    audio_query,
    audio_keys,
    audio_values,
    cross_video_query,
    cross_video_keys,
    cross_video_values,
    cross_audio_query,
    cross_audio_keys,
    cross_audio_values,
    video_length,
    audio_length,
    align_offset,
):
    devices = lax.axis_size("seq")
    index = lax.axis_index("seq")
    video_rows = video_query.shape[0]
    audio_rows = audio_query.shape[0]
    video_total = video_rows * devices
    audio_total = audio_rows * devices
    video_reach = video_total // 8
    audio_reach = 5 * audio_total // 8
    video_valid = video_length[0]
    audio_valid = audio_length[0]
    align_shift = align_offset[0]
    copies = max(devices // HV, 1)
    video_places = jnp.arange(video_total, dtype=jnp.int32)
    audio_places = jnp.arange(audio_total, dtype=jnp.int32)

    def video_open(q_where, k_where):
        return k_where < video_valid

    def toward_video(q_where, k_where):
        center = jnp.clip(q_where * audio_total // video_total + align_shift, 0, audio_valid - 1)
        return (k_where < audio_valid) & (jnp.abs(k_where - center) <= audio_reach)

    def toward_audio(q_where, k_where):
        center = jnp.clip((q_where - align_shift) * video_total // audio_total, 0, video_valid - 1)
        return (k_where < video_valid) & (jnp.abs(k_where - center) <= video_reach)

    video_owned = (
        lax.all_to_all(
            split_heads(video_query, HV, HDV, copies),
            "seq",
            split_axis=0,
            concat_axis=1,
            tiled=True,
        ),
        lax.all_to_all(
            spread_heads(video_keys, HV, HDV, copies),
            "seq",
            split_axis=0,
            concat_axis=1,
            tiled=True,
        ),
        lax.all_to_all(
            spread_heads(video_values, HV, HDV, copies),
            "seq",
            split_axis=0,
            concat_axis=1,
            tiled=True,
        ),
    )
    video_done = attend_local(
        video_owned[0],
        video_owned[1],
        video_owned[2],
        owned_positions(video_rows, copies, devices, index),
        video_places,
        video_open,
    )
    video_mixed = join_heads(
        lax.all_to_all(video_done, "seq", split_axis=1, concat_axis=0, tiled=True), HV, HDV, copies
    )
    audio_local = audio_query.reshape(audio_rows, HA, HDA)
    piece = (
        lax.all_gather(audio_keys, "seq", axis=0, tiled=True),
        lax.all_gather(audio_values, "seq", axis=0, tiled=True),
    )
    k_where = jnp.arange(piece[0].shape[0], dtype=jnp.int32)
    audio_k_where = k_where[None, :]
    permit = audio_k_where < audio_valid
    audio_state = fold_piece(
        fold_initial(audio_rows, HA, HDA), audio_local, piece[0], piece[1], permit, HA, HDA
    )
    audio_mixed = fold_finish(audio_state, HA, HDA)
    cross_owned = (
        lax.all_to_all(
            split_heads(cross_video_query, HA, HDA, copies),
            "seq",
            split_axis=0,
            concat_axis=1,
            tiled=True,
        ),
        lax.all_to_all(
            spread_heads(cross_audio_keys, HA, HDA, copies),
            "seq",
            split_axis=0,
            concat_axis=1,
            tiled=True,
        ),
        lax.all_to_all(
            spread_heads(cross_audio_values, HA, HDA, copies),
            "seq",
            split_axis=0,
            concat_axis=1,
            tiled=True,
        ),
    )
    cross_done = attend_local(
        cross_owned[0],
        cross_owned[1],
        cross_owned[2],
        owned_positions(video_rows, copies, devices, index),
        audio_places,
        toward_video,
    )
    video_cross = join_heads(
        lax.all_to_all(cross_done, "seq", split_axis=1, concat_axis=0, tiled=True), HA, HDA, copies
    )
    listen_owned = (
        lax.all_to_all(
            split_heads(cross_audio_query, HA, HDA, copies),
            "seq",
            split_axis=0,
            concat_axis=1,
            tiled=True,
        ),
        lax.all_to_all(
            spread_heads(cross_video_keys, HA, HDA, copies),
            "seq",
            split_axis=0,
            concat_axis=1,
            tiled=True,
        ),
        lax.all_to_all(
            spread_heads(cross_video_values, HA, HDA, copies),
            "seq",
            split_axis=0,
            concat_axis=1,
            tiled=True,
        ),
    )
    listen_done = attend_local(
        listen_owned[0],
        listen_owned[1],
        listen_owned[2],
        owned_positions(audio_rows, copies, devices, index),
        video_places,
        toward_audio,
    )
    audio_cross = join_heads(
        lax.all_to_all(listen_done, "seq", split_axis=1, concat_axis=0, tiled=True), HA, HDA, copies
    )
    return (video_mixed, audio_mixed, video_cross, audio_cross)


def solution(mesh):
    placed = (
        P(("clip", "seq"), None),
        P(("clip", "seq"), None),
        P(("clip", "seq"), None),
        P(("clip", "seq"), None),
        P(("clip", "seq"), None),
        P(("clip", "seq"), None),
        P(("clip", "seq"), None),
        P(("clip", "seq"), None),
        P(("clip", "seq"), None),
        P(("clip", "seq"), None),
        P(("clip", "seq"), None),
        P(("clip", "seq"), None),
        P("clip"),
        P("clip"),
        P("clip"),
    )
    return jax.shard_map(
        shards,
        mesh=mesh,
        in_specs=placed,
        out_specs=(
            P(("clip", "seq"), None),
            P(("clip", "seq"), None),
            P(("clip", "seq"), None),
            P(("clip", "seq"), None),
        ),
        check_vma=False,
    )
```

profile of v0, /device:TPU:0, one launch (start us, length us, event | category | flops | bytes accessed | tf_op | source)
XLA Modules:
  0.0 177.0 jit_solution(16282840157543856620)
XLA Ops:
  0.6 0.9 reshape.311
  1.6 0.7 reshape.329
  2.3 7.5 %all-to-all-start.8 = ((bf16[16,2,512]{2,1,0:T(2,128)(2,1)}), bf16[16,2,512]{2,1,0:T(2,128)(2,1)S(1)}, u32[]{:S(2)}, u32[]{:S(2)}) async-start(bf16[16,2,512]{2,1,0:T(2,128)(2,1)} %reshape.329), calls=%async_computation.8 | async-start | bytes 65536 | tf_op jit(solution)/shard_map/all_to_all | solution.py:240
  11.9 0.6 copy-done.7
  12.7 0.7 reshape.319
  13.7 0.7 reshape.321
  14.6 0.7 copy-done.9
  15.3 23.2 %all_gather.6 = bf16[128,2048]{1,0:T(8,128)(2,1)S(1)} all-gather(bf16[8,2048]{1,0:T(8,128)(2,1)S(1)} %copy-done.9), channel_id=1, replica_groups=mesh['clip'=2,'seq'=16] {'seq'}, dimensions={0}, use_global_device_ids=true | all-gather | bytes 557056 | tf_op jit(solution)/shard_map/all_gather | solution.py:195
  39.3 0.7 copy-done.10
  40.0 18.9 %all_gather.7 = bf16[128,2048]{1,0:T(8,128)(2,1)S(1)} all-gather(bf16[8,2048]{1,0:T(8,128)(2,1)S(1)} %copy-done.10), channel_id=1, replica_groups=mesh['clip'=2,'seq'=16] {'seq'}, dimensions={0}, use_global_device_ids=true | all-gather | bytes 557056 | tf_op jit(solution)/shard_map/all_gather | solution.py:196
  58.9 3.5 %all-to-all-start.5 = ((bf16[16,2,512]{2,1,0:T(2,128)(2,1)}), bf16[16,2,512]{2,1,0:T(2,128)(2,1)S(1)}, u32[]{:S(2)}, u32[]{:S(2)}) async-start(bf16[16,2,512]{2,1,0:T(2,128)(2,1)} %reshape.319), calls=%async_computation.5 | async-start | bytes 65536 | tf_op jit(solution)/shard_map/all_to_all | solution.py:213
  62.4 6.6 %all-to-all-done.5 = bf16[16,2,512]{2,1,0:T(2,128)(2,1)S(1)} async-done(((bf16[16,2,512]{2,1,0:T(2,128)(2,1)}), bf16[16,2,512]{2,1,0:T(2,128)(2,1)S(1)}, u32[]{:S(2)}, u32[]{:S(2)}) %all-to-all-start.5) | async-done | bytes 32800 | tf_op jit(solution)/shard_map/all_to_all | solution.py:213
  69.0 3.5 %all-to-all-start.6 = ((bf16[16,2,512]{2,1,0:T(2,128)(2,1)}), bf16[16,2,512]{2,1,0:T(2,128)(2,1)S(1)}, u32[]{:S(2)}, u32[]{:S(2)}) async-start(bf16[16,2,512]{2,1,0:T(2,128)(2,1)} %reshape.321), calls=%async_computation.6 | async-start | bytes 65536 | tf_op jit(solution)/shard_map/all_to_all | solution.py:220
  72.6 0.7 copy.128
  73.6 0.7 copy.130
  74.5 0.8 copy-done.3
  75.5 0.8 reshape.317
  76.3 2.8 %all-to-all-done.6 = bf16[16,2,512]{2,1,0:T(2,128)(2,1)S(1)} async-done(((bf16[16,2,512]{2,1,0:T(2,128)(2,1)}), bf16[16,2,512]{2,1,0:T(2,128)(2,1)S(1)}, u32[]{:S(2)}, u32[]{:S(2)}) %all-to-all-start.6) | async-done | bytes 32800 | tf_op jit(solution)/shard_map/all_to_all | solution.py:220
  79.1 3.5 %all-to-all-start.4 = ((bf16[16,2,1024]{2,1,0:T(2,128)(2,1)}), bf16[16,2,1024]{2,1,0:T(2,128)(2,1)S(1)}, u32[]{:S(2)}, u32[]{:S(2)}) async-start(bf16[16,2,1024]{2,1,0:T(2,128)(2,1)} %reshape.317), calls=%async_computation.4 | async-start | bytes 131072 | tf_op jit(solution)/shard_map/all_to_all | solution.py:206
  82.6 0.7 copy.132
  83.7 0.8 reshape.327
  84.8 0.8 reshape.325
  86.1 3.4 %all-to-all-done.4 = bf16[16,2,1024]{2,1,0:T(2,128)(2,1)S(1)} async-done(((bf16[16,2,1024]{2,1,0:T(2,128)(2,1)}), bf16[16,2,1024]{2,1,0:T(2,128)(2,1)S(1)}, u32[]{:S(2)}, u32[]{:S(2)}) %all-to-all-start.4) | async-done | bytes 65568 | tf_op jit(solution)/shard_map/all_to_all | solution.py:206
  89.5 3.5 %all-to-all-start.9 = ((bf16[16,2,1024]{2,1,0:T(2,128)(2,1)}), bf16[16,2,1024]{2,1,0:T(2,128)(2,1)S(1)}, u32[]{:S(2)}, u32[]{:S(2)}) async-start(bf16[16,2,1024]{2,1,0:T(2,128)(2,1)} %reshape.327), calls=%async_computation.9 | async-start | bytes 131072 | tf_op jit(solution)/shard_map/all_to_all | solution.py:247
  93.4 6.4 %all-to-all-done.9 = bf16[16,2,1024]{2,1,0:T(2,128)(2,1)S(1)} async-done(((bf16[16,2,1024]{2,1,0:T(2,128)(2,1)}), bf16[16,2,1024]{2,1,0:T(2,128)(2,1)S(1)}, u32[]{:S(2)}, u32[]{:S(2)}) %all-to-all-start.9) | async-done | bytes 65568 | tf_op jit(solution)/shard_map/all_to_all | solution.py:247
  99.8 3.5 %all-to-all-start.10 = ((bf16[16,2,1024]{2,1,0:T(2,128)(2,1)}), bf16[16,2,1024]{2,1,0:T(2,128)(2,1)S(1)}, u32[]{:S(2)}, u32[]{:S(2)}) async-start(bf16[16,2,1024]{2,1,0:T(2,128)(2,1)} %reshape.325), calls=%async_computation.10 | async-start | bytes 131072 | tf_op jit(solution)/shard_map/all_to_all | solution.py:254
  103.8 6.4 %all-to-all-done.10 = bf16[16,2,1024]{2,1,0:T(2,128)(2,1)S(1)} async-done(((bf16[16,2,1024]{2,1,0:T(2,128)(2,1)}), bf16[16,2,1024]{2,1,0:T(2,128)(2,1)S(1)}, u32[]{:S(2)}, u32[]{:S(2)}) %all-to-all-start.10) | async-done | bytes 65568 | tf_op jit(solution)/shard_map/all_to_all | solution.py:254
  110.2 3.5 %all-to-all-start = ((bf16[32,16,128]{2,1,0:T(8,128)(2,1)}), bf16[32,16,128]{2,1,0:T(8,128)(2,1)S(1)}, u32[]{:S(2)}, u32[]{:S(2)}) async-start(bf16[32,16,128]{2,1,0:T(8,128)(2,1)} %copy.128), calls=%async_computation | async-start | bytes 262144 | tf_op jit(solution)/shard_map/all_to_all | solution.py:160
  114.1 7.5 %all-to-all-done = bf16[32,16,128]{2,1,0:T(8,128)(2,1)S(1)} async-done(((bf16[32,16,128]{2,1,0:T(8,128)(2,1)}), bf16[32,16,128]{2,1,0:T(8,128)(2,1)S(1)}, u32[]{:S(2)}, u32[]{:S(2)}) %all-to-all-start) | async-done | bytes 131104 | tf_op jit(solution)/shard_map/all_to_all | solution.py:160
  121.6 3.5 %all-to-all-start.1 = ((bf16[32,16,128]{2,1,0:T(8,128)(2,1)}), bf16[32,16,128]{2,1,0:T(8,128)(2,1)S(1)}, u32[]{:S(2)}, u32[]{:S(2)}) async-start(bf16[32,16,128]{2,1,0:T(8,128)(2,1)} %copy.130), calls=%async_computation.1 | async-start | bytes 262144 | tf_op jit(solution)/shard_map/all_to_all | solution.py:167
  125.2 0.8 reshape.323
  126.6 0.7 reshape.331
  127.3 5.7 %all-to-all-done.1 = bf16[32,16,128]{2,1,0:T(8,128)(2,1)S(1)} async-done(((bf16[32,16,128]{2,1,0:T(8,128)(2,1)}), bf16[32,16,128]{2,1,0:T(8,128)(2,1)S(1)}, u32[]{:S(2)}, u32[]{:S(2)}) %all-to-all-start.1) | async-done | bytes 131104 | tf_op jit(solution)/shard_map/all_to_all | solution.py:167
  133.0 3.5 %all-to-all-start.2 = ((bf16[32,16,128]{2,1,0:T(8,128)(2,1)}), bf16[32,16,128]{2,1,0:T(8,128)(2,1)S(1)}, u32[]{:S(2)}, u32[]{:S(2)}) async-start(bf16[32,16,128]{2,1,0:T(8,128)(2,1)} %copy.132), calls=%async_computation.2 | async-start | bytes 262144 | tf_op jit(solution)/shard_map/all_to_all | solution.py:174
  136.9 7.5 %all-to-all-done.2 = bf16[32,16,128]{2,1,0:T(8,128)(2,1)S(1)} async-done(((bf16[32,16,128]{2,1,0:T(8,128)(2,1)}), bf16[32,16,128]{2,1,0:T(8,128)(2,1)S(1)}, u32[]{:S(2)}, u32[]{:S(2)}) %all-to-all-start.2) | async-done | bytes 131104 | tf_op jit(solution)/shard_map/all_to_all | solution.py:174
  144.4 3.5 %all-to-all-start.11 = ((bf16[16,2,512]{2,1,0:T(2,128)(2,1)}), bf16[16,2,512]{2,1,0:T(2,128)(2,1)S(1)}, u32[]{:S(2)}, u32[]{:S(2)}) async-start(bf16[16,2,512]{2,1,0:T(2,128)(2,1)} %reshape.331), calls=%async_computation.11 | async-start | bytes 65536 | tf_op jit(solution)/shard_map/all_to_all | solution.py:271
  147.9 6.6 %all-to-all-done.11 = bf16[16,2,512]{2,1,0:T(2,128)(2,1)S(1)} async-done(((bf16[16,2,512]{2,1,0:T(2,128)(2,1)}), bf16[16,2,512]{2,1,0:T(2,128)(2,1)S(1)}, u32[]{:S(2)}, u32[]{:S(2)}) %all-to-all-start.11) | async-done | bytes 32800 | tf_op jit(solution)/shard_map/all_to_all | solution.py:271
  154.5 3.5 %all-to-all-start.7 = ((bf16[16,2,1024]{2,1,0:T(2,128)(2,1)}), bf16[16,2,1024]{2,1,0:T(2,128)(2,1)S(1)}, u32[]{:S(2)}, u32[]{:S(2)}) async-start(bf16[16,2,1024]{2,1,0:T(2,128)(2,1)} %reshape.323), calls=%async_computation.7 | async-start | bytes 131072 | tf_op jit(solution)/shard_map/all_to_all | solution.py:237
  158.0 0.4 fusion.4
  158.4 0.8 copy.135
  159.2 5.7 %all-to-all-done.7 = bf16[16,2,1024]{2,1,0:T(2,128)(2,1)S(1)} async-done(((bf16[16,2,1024]{2,1,0:T(2,128)(2,1)}), bf16[16,2,1024]{2,1,0:T(2,128)(2,1)S(1)}, u32[]{:S(2)}, u32[]{:S(2)}) %all-to-all-start.7) | async-done | bytes 65568 | tf_op jit(solution)/shard_map/all_to_all | solution.py:237
  164.8 3.5 %all-to-all-start.3 = ((bf16[2,256,128]{2,0,1:T(2,128)(2,1)}), bf16[2,256,128]{2,0,1:T(2,128)(2,1)S(1)}, u32[]{:S(2)}, u32[]{:S(2)}) async-start(bf16[2,256,128]{2,0,1:T(2,128)(2,1)} %copy.135), calls=%async_computation.3 | async-start | bytes 262144 | tf_op jit(solution)/shard_map/all_to_all | solution.py:191
  168.7 0.4 fusion.10
  169.1 0.7 reshape.304
  170.0 0.7 reshape.316
  171.0 0.8 reshape.310
  171.8 4.4 %all-to-all-done.3 = bf16[2,256,128]{2,0,1:T(2,128)(2,1)S(1)} async-done(((bf16[2,256,128]{2,0,1:T(2,128)(2,1)}), bf16[2,256,128]{2,0,1:T(2,128)(2,1)S(1)}, u32[]{:S(2)}, u32[]{:S(2)}) %all-to-all-start.3) | async-done | bytes 131104 | tf_op jit(solution)/shard_map/all_to_all | solution.py:191
  176.3 0.7 copy.204
  (87 shorter events, 6.4 us)
Async XLA Ops:
  2.3 9.5 %copy-start.6 = (bf16[8,2048]{1,0:T(8,128)(2,1)S(1)}, bf16[8,2048]{1,0:T(8,128)(2,1)}, u32[]{:S(2)}) copy-start(bf16[8,2048]{1,0:T(8,128)(2,1)} %param.18) | copy-start | bytes 98308
  2.3 56.6 %all-to-all-start.8 = ((bf16[16,2,512]{2,1,0:T(2,128)(2,1)}), bf16[16,2,512]{2,1,0:T(2,128)(2,1)S(1)}, u32[]{:S(2)}, u32[]{:S(2)}) async-start(bf16[16,2,512]{2,1,0:T(2,128)(2,1)} %reshape.329), calls=%async_computation.8 | async-start | bytes 65536 | tf_op jit(solution)/shard_map/all_to_all | solution.py:240
  11.8 0.8 copy-start.7
  12.7 0.8 copy-start.8
  13.6 0.9 copy-start
  14.5 0.8 copy-start.9
  39.3 0.8 copy-start.10
  58.9 10.1 %all-to-all-start.5 = ((bf16[16,2,512]{2,1,0:T(2,128)(2,1)}), bf16[16,2,512]{2,1,0:T(2,128)(2,1)S(1)}, u32[]{:S(2)}, u32[]{:S(2)}) async-start(bf16[16,2,512]{2,1,0:T(2,128)(2,1)} %reshape.319), calls=%async_computation.5 | async-start | bytes 65536 | tf_op jit(solution)/shard_map/all_to_all | solution.py:213
  69.0 10.1 %all-to-all-start.6 = ((bf16[16,2,512]{2,1,0:T(2,128)(2,1)}), bf16[16,2,512]{2,1,0:T(2,128)(2,1)S(1)}, u32[]{:S(2)}, u32[]{:S(2)}) async-start(bf16[16,2,512]{2,1,0:T(2,128)(2,1)} %reshape.321), calls=%async_computation.6 | async-start | bytes 65536 | tf_op jit(solution)/shard_map/all_to_all | solution.py:220
  72.6 0.9 copy-start.1
  73.6 0.9 copy-start.2
  74.5 0.8 copy-start.3
  79.1 10.4 %all-to-all-start.4 = ((bf16[16,2,1024]{2,1,0:T(2,128)(2,1)}), bf16[16,2,1024]{2,1,0:T(2,128)(2,1)S(1)}, u32[]{:S(2)}, u32[]{:S(2)}) async-start(bf16[16,2,1024]{2,1,0:T(2,128)(2,1)} %reshape.317), calls=%async_computation.4 | async-start | bytes 131072 | tf_op jit(solution)/shard_map/all_to_all | solution.py:206
  82.6 0.8 copy-start.4
  83.7 0.8 copy-start.5
  89.5 10.3 %all-to-all-start.9 = ((bf16[16,2,1024]{2,1,0:T(2,128)(2,1)}), bf16[16,2,1024]{2,1,0:T(2,128)(2,1)S(1)}, u32[]{:S(2)}, u32[]{:S(2)}) async-start(bf16[16,2,1024]{2,1,0:T(2,128)(2,1)} %reshape.327), calls=%async_computation.9 | async-start | bytes 131072 | tf_op jit(solution)/shard_map/all_to_all | solution.py:247
  99.8 10.4 %all-to-all-start.10 = ((bf16[16,2,1024]{2,1,0:T(2,128)(2,1)}), bf16[16,2,1024]{2,1,0:T(2,128)(2,1)S(1)}, u32[]{:S(2)}, u32[]{:S(2)}) async-start(bf16[16,2,1024]{2,1,0:T(2,128)(2,1)} %reshape.325), calls=%async_computation.10 | async-start | bytes 131072 | tf_op jit(solution)/shard_map/all_to_all | solution.py:254
  110.2 11.4 %all-to-all-start = ((bf16[32,16,128]{2,1,0:T(8,128)(2,1)}), bf16[32,16,128]{2,1,0:T(8,128)(2,1)S(1)}, u32[]{:S(2)}, u32[]{:S(2)}) async-start(bf16[32,16,128]{2,1,0:T(8,128)(2,1)} %copy.128), calls=%async_computation | async-start | bytes 262144 | tf_op jit(solution)/shard_map/all_to_all | solution.py:160
  121.6 11.4 %all-to-all-start.1 = ((bf16[32,16,128]{2,1,0:T(8,128)(2,1)}), bf16[32,16,128]{2,1,0:T(8,128)(2,1)S(1)}, u32[]{:S(2)}, u32[]{:S(2)}) async-start(bf16[32,16,128]{2,1,0:T(8,128)(2,1)} %copy.130), calls=%async_computation.1 | async-start | bytes 262144 | tf_op jit(solution)/shard_map/all_to_all | solution.py:167
  133.0 11.4 %all-to-all-start.2 = ((bf16[32,16,128]{2,1,0:T(8,128)(2,1)}), bf16[32,16,128]{2,1,0:T(8,128)(2,1)S(1)}, u32[]{:S(2)}, u32[]{:S(2)}) async-start(bf16[32,16,128]{2,1,0:T(8,128)(2,1)} %copy.132), calls=%async_computation.2 | async-start | bytes 262144 | tf_op jit(solution)/shard_map/all_to_all | solution.py:174
  144.4 10.1 %all-to-all-start.11 = ((bf16[16,2,512]{2,1,0:T(2,128)(2,1)}), bf16[16,2,512]{2,1,0:T(2,128)(2,1)S(1)}, u32[]{:S(2)}, u32[]{:S(2)}) async-start(bf16[16,2,512]{2,1,0:T(2,128)(2,1)} %reshape.331), calls=%async_computation.11 | async-start | bytes 65536 | tf_op jit(solution)/shard_map/all_to_all | solution.py:271
  154.5 10.4 %all-to-all-start.7 = ((bf16[16,2,1024]{2,1,0:T(2,128)(2,1)}), bf16[16,2,1024]{2,1,0:T(2,128)(2,1)S(1)}, u32[]{:S(2)}, u32[]{:S(2)}) async-start(bf16[16,2,1024]{2,1,0:T(2,128)(2,1)} %reshape.323), calls=%async_computation.7 | async-start | bytes 131072 | tf_op jit(solution)/shard_map/all_to_all | solution.py:237
  164.8 11.4 %all-to-all-start.3 = ((bf16[2,256,128]{2,0,1:T(2,128)(2,1)}), bf16[2,256,128]{2,0,1:T(2,128)(2,1)S(1)}, u32[]{:S(2)}, u32[]{:S(2)}) async-start(bf16[2,256,128]{2,0,1:T(2,128)(2,1)} %copy.135), calls=%async_computation.3 | async-start | bytes 262144 | tf_op jit(solution)/shard_map/all_to_all | solution.py:191
where the time goes:
time: 179 us; the launch traced here: 177 us
  waiting for transfers between devices  62.8 us (35%)
  starting transfers between devices  46.1 us (26%)
  blocking collectives  42.1 us (24%)
  local copies, waits for them, and re-layouts  19.7 us (11%)
  between operations  3.15 us (2%)
  matrix products  2.36 us (1%)
    all_gather x1, blocking collectives, shards(): lax.all_gather(audio_keys, 'seq', axis=0, tiled=True)  23.2 us
    all_gather x1, blocking collectives, shards(): lax.all_gather(audio_values, 'seq', axis=0, tiled=True)  18.9 us
    unnamed x42, local copies, waits for them, and re-layouts  11.4 us
    all_to_all x1, starting transfers between devices, shards(): lax.all_to_all(split_heads(cross_audio_query, HA, HDA, copies), 'seq', sp...  7.55 us
    all_to_all x1, waiting for transfers between devices, shards(): lax.all_to_all(spread_heads(video_values, HV, HDV, copies), 'seq', split_...  7.46 us
    all_to_all x1, waiting for transfers between devices, shards(): lax.all_to_all(split_heads(video_query, HV, HDV, copies), 'seq', split_ax...  7.46 us
    all_to_all x1, waiting for transfers between devices, shards(): lax.all_to_all(spread_heads(cross_audio_keys, HA, HDA, copies), 'seq', sp...  6.57 us
    all_to_all x1, waiting for transfers between devices, shards(): lax.all_to_all(listen_done, 'seq', split_axis=1, concat_axis=0, tiled=True)  6.56 us
  transfers between devices with their start and end apart: 12, of which 11 were waited for; matrix products, arithmetic and copies ran while one was open for 9% of the time, Pallas kernels for 0%

commit v1 on v0

--- a/solution.py
+++ b/solution.py
@@ -1,8 +1,11 @@
+import functools
 import math
 
 import jax
 import jax.numpy as jnp
 from jax import lax
+from jax.experimental import pallas as pl
+from jax.experimental.pallas import tpu as pltpu
 from jax.sharding import PartitionSpec as P
 
 HV = 32
@@ -273,6 +276,209 @@
     return (video_mixed, audio_mixed, video_cross, audio_cross)
 
 
+LANES = 128
+
+GROUPS = ((0, 1, 2), (6, 10, 11), (9, 7, 8), (3, 4, 5))
+OUT_OF_GROUP = (0, 2, 3, 1)
+
+
+def softmax_mix(query, keys, values, permit, scale):
+    scores = lax.dot_general(
+        query, keys, (((1,), (1,)), ((), ())), preferred_element_type=jnp.float32
+    )
+    scores = jnp.where(permit, scores * scale, -1e30)
+    peak = jnp.max(scores, axis=1, keepdims=True)
+    weights = jnp.exp(scores - peak)
+    total = jnp.sum(weights, axis=1, keepdims=True)
+    mixed = jnp.dot(weights.astype(jnp.bfloat16), values, preferred_element_type=jnp.float32)
+    return mixed / total
+
+
+def read_tokens(ref, column):
+    block = ref[:, :, column : column + LANES]
+    n, rows, _ = block.shape
+    if rows % 16:
+        return block.astype(jnp.float32).reshape(n * rows, LANES).astype(block.dtype)
+    return block.reshape(n * rows, LANES)
+
+
+def write_tokens(ref, column, result):
+    n, rows, _ = ref.shape
+    ref[:, :, column : column + LANES] = result.reshape(n, rows, LANES).astype(ref.dtype)
+
+
+def fused_kernel(n, ratio, *refs):
+    video_length, audio_length, align_offset = refs[:3]
+    arrays = refs[3:15]
+    outs = refs[15:19]
+    held = refs[19:31]
+    results = refs[31:35]
+    send_sem, recv_sem, back_send, back_recv = refs[35:]
+    me = lax.axis_index("seq")
+
+    def columns(width, owner):
+        return pl.ds(pl.multiple_of(owner * width, LANES), width)
+
+    own = []
+    for group in GROUPS:
+        for at in group:
+            width = held[at].shape[2]
+            copy = pltpu.make_async_copy(
+                arrays[at].at[:, columns(width, me)], held[at].at[me], recv_sem.at[at]
+            )
+            own.append(copy)
+            copy.start()
+
+    barrier = pltpu.get_barrier_semaphore()
+
+    @pl.loop(1, n)
+    def _(step):
+        pl.semaphore_signal(
+            barrier,
+            inc=1,
+            device_id={"seq": lax.rem(me + step, n)},
+            device_id_type=pl.DeviceIdType.MESH,
+        )
+
+    pl.semaphore_wait(barrier, n - 1)
+
+    for group in GROUPS:
+
+        @pl.loop(1, n)
+        def _(step, group=group):
+            peer = lax.rem(me + step, n)
+            for at in group:
+                width = held[at].shape[2]
+                pltpu.make_async_remote_copy(
+                    src_ref=arrays[at].at[:, columns(width, peer)],
+                    dst_ref=held[at].at[me],
+                    send_sem=send_sem.at[at],
+                    recv_sem=recv_sem.at[at],
+                    device_id={"seq": peer},
+                    device_id_type=pl.DeviceIdType.MESH,
+                ).start()
+
+    video_valid = video_length[0]
+    audio_valid = audio_length[0]
+    shift = align_offset[0]
+    video_total = n * held[0].shape[1]
+    audio_total = n * held[3].shape[1]
+    video_reach = video_total // 8
+    audio_reach = 5 * audio_total // 8
+
+    def places(count, copies):
+        rows = lax.broadcasted_iota(jnp.int32, (count, 1), 0)
+        return jnp.concatenate([rows] * copies, axis=0)
+
+    def key_places(count):
+        return lax.broadcasted_iota(jnp.int32, (1, count), 1)
+
+    def permit_of(which, copies):
+        if which == 0:
+            return key_places(video_total) < video_valid
+        if which == 1:
+            return key_places(audio_total) < audio_valid
+        if which == 2:
+            where = key_places(audio_total)
+            spots = lax.shift_right_logical(places(video_total, copies), ratio.bit_length() - 1)
+            center = jnp.clip(spots + shift, 0, audio_valid - 1)
+            return (where < audio_valid) & (jnp.abs(where - center) <= audio_reach)
+        where = key_places(video_total)
+        spots = (places(audio_total, copies) - shift) * ratio
+        center = jnp.clip(spots, 0, video_valid - 1)
+        return (where < video_valid) & (jnp.abs(where - center) <= video_reach)
+
+    for group, which in zip(GROUPS, OUT_OF_GROUP):
+        for at in group:
+            pltpu.make_async_copy(held[at], held[at], recv_sem.at[at]).wait()
+        query, keys, values = (held[at] for at in group)
+        depth = HDV if which == 0 else HDA
+        copies = LANES // depth
+        scale = 1.0 / math.sqrt(depth)
+        permit = permit_of(which, copies)
+        for column in range(0, query.shape[2], LANES):
+            tokens = read_tokens(query, column)
+            if copies > 1:
+                lane = lax.broadcasted_iota(jnp.int32, tokens.shape, 1) // depth
+                zero = jnp.zeros_like(tokens)
+                tokens = jnp.concatenate(
+                    [jnp.where(lane == head, tokens, zero) for head in range(copies)], axis=0
+                )
+            mixed = softmax_mix(
+                tokens, read_tokens(keys, column), read_tokens(values, column), permit, scale
+            )
+            if copies > 1:
+                rows = mixed.shape[0] // copies
+                merged = mixed[:rows]
+                lane = lax.broadcasted_iota(jnp.int32, merged.shape, 1) // depth
+                for head in range(1, copies):
+                    merged = jnp.where(lane == head, mixed[head * rows : (head + 1) * rows], merged)
+                mixed = merged
+            write_tokens(results[which], column, mixed)
+        width = results[which].shape[2]
+        target = outs[which].at[:, columns(width, me)]
+        pltpu.make_async_copy(results[which].at[me], target, back_recv.at[which]).start()
+
+        @pl.loop(1, n)
+        def _(step, which=which, target=target):
+            peer = lax.rem(me + step, n)
+            pltpu.make_async_remote_copy(
+                src_ref=results[which].at[peer],
+                dst_ref=target,
+                send_sem=back_send.at[which],
+                recv_sem=back_recv.at[which],
+                device_id={"seq": peer},
+                device_id_type=pl.DeviceIdType.MESH,
+            ).start()
+
+    for at in range(12):
+        part = held[at].at[pl.ds(0, n - 1)]
+        pltpu.make_async_copy(part, part, send_sem.at[at]).wait()
+    for which in range(4):
+        part = results[which].at[pl.ds(0, n - 1)]
+        pltpu.make_async_copy(part, part, back_send.at[which]).wait()
+        pltpu.make_async_copy(outs[which], outs[which], back_recv.at[which]).wait()
+
+
+def fused_shards(*arguments):
+    n = lax.axis_size("seq")
+    arrays = arguments[:12]
+    lengths = arguments[12:]
+    ratio = arrays[0].shape[0] // arrays[3].shape[0]
+    held = [pltpu.VMEM((n, a.shape[0], a.shape[1] // n), a.dtype) for a in arrays]
+    results = [held[at] for at in (0, 3, 6, 9)]
+    outs = tuple(jax.ShapeDtypeStruct(arrays[at].shape, arrays[at].dtype) for at in (0, 3, 6, 9))
+    anywhere = pl.BlockSpec(memory_space=pl.ANY)
+    scalars = pl.BlockSpec(memory_space=pltpu.SMEM)
+    return pl.pallas_call(
+        functools.partial(fused_kernel, n, ratio),
+        out_shape=outs,
+        in_specs=[scalars] * 3 + [anywhere] * 12,
+        out_specs=(anywhere,) * 4,
+        scratch_shapes=held
+        + results
+        + [
+            pltpu.SemaphoreType.DMA((12,)),
+            pltpu.SemaphoreType.DMA((12,)),
+            pltpu.SemaphoreType.DMA((4,)),
+            pltpu.SemaphoreType.DMA((4,)),
+        ],
+        compiler_params=pltpu.CompilerParams(collective_id=0, has_side_effects=True),
+    )(*lengths, *arrays)
+
+
+def kernel_fits(n, video_rows, audio_rows):
+    if n < 2 or HV % n or HA % n or (HV // n * HDV) % LANES or (HA // n * HDA) % LANES:
+        return False
+    ratio = video_rows // audio_rows
+    return video_rows == ratio * audio_rows and ratio & (ratio - 1) == 0 and audio_rows % 8 == 0
+
+
+def dispatch(*arguments):
+    fits = kernel_fits(lax.axis_size("seq"), arguments[0].shape[0], arguments[3].shape[0])
+    return (fused_shards if fits else shards)(*arguments)
+
+
 def solution(mesh):
     placed = (
         P(("clip", "seq"), None),
@@ -292,7 +498,7 @@
         P("clip"),
     )
     return jax.shard_map(
-        shards,
+        dispatch,
         mesh=mesh,
         in_specs=placed,
         out_specs=(

time: 179 us -> 39.7 us (0.22)
  waiting for transfers between devices: 62.8 us -> 0 us
  starting transfers between devices: 46.1 us -> 0 us
  blocking collectives: 42.1 us -> 0 us
  Pallas kernels: 0 us -> 33 us
  local copies, waits for them, and re-layouts: 19.7 us -> 3.8 us
  matrix products: 2.36 us -> 0 us
    all_to_all x12 -> x0, waiting for transfers between devices: 62.8 us -> none  [the longest x1 7.46 us: shards(): lax.all_to_all(spread_heads(video_values, HV, HDV, copies), 'seq', split_...]
    all_to_all x12 -> x0, starting transfers between devices: 46.1 us -> none  [the longest x1 7.55 us: shards(): lax.all_to_all(split_heads(cross_audio_query, HA, HDA, copies), 'seq', sp...]
    all_gather x2 -> x0, blocking collectives: 42.1 us -> none  [the longest x1 23.2 us: shards(): lax.all_gather(audio_keys, 'seq', axis=0, tiled=True)]
    pallas_call x0 -> x1, Pallas kernels: none -> 33 us  [fused_shards(): pl.pallas_call(functools.partial(fused_kernel, n, ratio), out_shape=outs,...]
    unnamed x42 -> x10, local copies, waits for them, and re-layouts: 11.4 us -> 3.8 us
    reshape x14 -> x0, local copies, waits for them, and re-layouts: 4.87 us -> none  [the longest x2 1.55 us: join_heads(): return shaped.reshape(copies * part_rows, heads * depth)]
    dot_general x8 -> x0, matrix products: 2.36 us -> none  [the longest x4 1.31 us: online_update(): jnp.einsum(value_form, weights.astype(jnp.bfloat16), value_tile, preferre...]
  transfers between devices with their start and end apart: 12 -> 0, of which waited for: 11 -> 0; matrix products, arithmetic and copies ran while one was open for 9% -> 0% of each run, Pallas kernels for 0% -> 0%
where the time goes in v1:
time: 39.7 us; the launch traced here: 39.4 us
  Pallas kernels  33 us (83%)
  local copies, waits for them, and re-layouts  3.8 us (10%)
  between operations  2.59 us (7%)
    pallas_call x1, Pallas kernels, fused_shards(): pl.pallas_call(functools.partial(fused_kernel, n, ratio), out_shape=outs,...  33 us
    unnamed x10, local copies, waits for them, and re-layouts  3.8 us

profile of v1, /device:TPU:0, one launch (start us, length us, event | category | flops | bytes accessed | tf_op | source)
XLA Modules:
  0.0 39.4 jit_solution(10998742007762994980)
XLA Ops:
  2.6 33.0 %shard_map.174 = (bf16[16,4096]{1,0:T(8,128)(2,1)}, bf16[8,2048]{1,0:T(8,128)(2,1)}, bf16[16,2048]{1,0:T(8,128)(2,1)}, bf16[8,2048]{1,0:T(8,128)(2,1)}) custom-call(s32[1]{0:T(128)S(6)} %copy.23.refs_0_, s32[1]{0:T(128)S(6)} %copy.24.refs_1_, s32[1]{0:T(128)S(6)} %copy.25.refs_2_, bf16[16,4096]{1,0:T(8,128)(2,1)} %refs_3_.1, bf16[16,4096]{1,0:T(8,128)(2,1)} %refs_4_.1, ...), custom_call_target="tpu_custom_call" | custom-call | tf_op jit(solution)/shard_map/pallas_call | solution.py:453
  35.6 0.0 copy-start.2
  35.6 1.6 %copy.26 = bf16[16,4096]{1,0:T(8,128)(2,1)} copy(bf16[16,4096]{1,0:T(8,128)(2,1)} %get-tuple-element.8) | data formatting | bytes 262144
  37.2 0.0 copy-done.2
  37.2 0.0 copy-start
  37.2 0.6 %copy.27 = bf16[8,2048]{1,0:T(8,128)(2,1)} copy(bf16[8,2048]{1,0:T(8,128)(2,1)S(1)} %copy-done.2) | data formatting | bytes 65536
  37.8 0.2 copy-done
  38.0 0.0 copy-start.1
  38.0 0.6 %copy.28 = bf16[16,2048]{1,0:T(8,128)(2,1)} copy(bf16[16,2048]{1,0:T(8,128)(2,1)S(1)} %copy-done) | data formatting | bytes 131072
  38.6 0.1 copy-done.1
  38.8 0.6 %copy.29 = bf16[8,2048]{1,0:T(8,128)(2,1)} copy(bf16[8,2048]{1,0:T(8,128)(2,1)S(1)} %copy-done.1) | data formatting | bytes 65536
Async XLA Ops:
  35.6 1.6 %copy-start.2 = (bf16[8,2048]{1,0:T(8,128)(2,1)S(1)}, bf16[8,2048]{1,0:T(8,128)(2,1)}, u32[]{:S(2)}) copy-start(bf16[8,2048]{1,0:T(8,128)(2,1)} %get-tuple-element.9) | copy-start | bytes 98308
  37.2 0.9 %copy-start = (bf16[16,2048]{1,0:T(8,128)(2,1)S(1)}, bf16[16,2048]{1,0:T(8,128)(2,1)}, u32[]{:S(2)}) copy-start(bf16[16,2048]{1,0:T(8,128)(2,1)} %get-tuple-element.10) | copy-start | bytes 196612
  38.0 0.8 %copy-start.1 = (bf16[8,2048]{1,0:T(8,128)(2,1)S(1)}, bf16[8,2048]{1,0:T(8,128)(2,1)}, u32[]{:S(2)}) copy-start(bf16[8,2048]{1,0:T(8,128)(2,1)} %get-tuple-element.11) | copy-start | bytes 98308

commit v2 on v1

--- a/solution.py
+++ b/solution.py
@@ -278,8 +278,12 @@
 
 LANES = 128
 
-GROUPS = ((0, 1, 2), (6, 10, 11), (9, 7, 8), (3, 4, 5))
-OUT_OF_GROUP = (0, 2, 3, 1)
+GROUPS = (
+    ((0, 1, 2), 0, False),
+    ((3, 4, 5), 1, False),
+    ((9, 7, 8), 3, True),
+    ((6, 10, 11), 2, True),
+)
 
 
 def softmax_mix(query, keys, values, permit, scale):
@@ -307,27 +311,66 @@
     ref[:, :, column : column + LANES] = result.reshape(n, rows, LANES).astype(ref.dtype)
 
 
+def margin_blocks(n, video_rows):
+    return min(-(-(3 * n * video_rows // 16) // video_rows), n // 2)
+
+
+def held_shapes(n, arrays):
+    half = n // 2
+    shapes = [None] * 12
+    for group, which, halved in GROUPS:
+        for place, at in enumerate(group):
+            rows, cols = arrays[at].shape
+            blocks = n
+            if halved and place == 0:
+                blocks = half
+            elif which == 3:
+                blocks = half + margin_blocks(n, rows)
+            shapes[at] = (blocks, rows, cols // (half if halved else n))
+    return shapes
+
+
 def fused_kernel(n, ratio, *refs):
     video_length, audio_length, align_offset = refs[:3]
     arrays = refs[3:15]
     outs = refs[15:19]
     held = refs[19:31]
     results = refs[31:35]
-    send_sem, recv_sem, back_send, back_recv = refs[35:]
+    send_sem, far_sem, recv_sem, back_send, back_recv = refs[35:]
+    half = n // 2
+    margin = held[7].shape[0] - half
     me = lax.axis_index("seq")
+    side = me // half
+    inner = lax.rem(me, half)
+    near = (me >= half - margin) & (me < half + margin)
 
     def columns(width, owner):
         return pl.ds(pl.multiple_of(owner * width, LANES), width)
 
-    own = []
-    for group in GROUPS:
+    def slot_of(group, which, halved, at, to_side):
+        if halved and at == group[0]:
+            return inner
+        if which == 3:
+            return me - to_side * (half - margin)
+        return me
+
+    def send(at, owner, slot, peer, sem):
+        pltpu.make_async_remote_copy(
+            src_ref=arrays[at].at[:, columns(held[at].shape[2], owner)],
+            dst_ref=held[at].at[slot],
+            send_sem=sem.at[at],
+            recv_sem=recv_sem.at[at],
+            device_id={"seq": peer},
+            device_id_type=pl.DeviceIdType.MESH,
+        ).start()
+
+    for group, which, halved in GROUPS:
         for at in group:
-            width = held[at].shape[2]
-            copy = pltpu.make_async_copy(
-                arrays[at].at[:, columns(width, me)], held[at].at[me], recv_sem.at[at]
-            )
-            own.append(copy)
-            copy.start()
+            pltpu.make_async_copy(
+                arrays[at].at[:, columns(held[at].shape[2], inner if halved else me)],
+                held[at].at[slot_of(group, which, halved, at, side)],
+                recv_sem.at[at],
+            ).start()
 
     barrier = pltpu.get_barrier_semaphore()
 
@@ -342,32 +385,55 @@
 
     pl.semaphore_wait(barrier, n - 1)
 
-    for group in GROUPS:
-
-        @pl.loop(1, n)
-        def _(step, group=group):
-            peer = lax.rem(me + step, n)
+    for group, which, halved in GROUPS:
+        if not halved:
+
+            @pl.loop(0, half)
+            def _(step, group=group):
+                peer = (1 - side) * half + lax.rem(inner + step, half)
+                for at in group:
+                    send(at, peer, me, peer, far_sem)
+
+            @pl.loop(1, half)
+            def _(step, group=group):
+                peer = side * half + lax.rem(inner + step, half)
+                for at in group:
+                    send(at, peer, me, peer, send_sem)
+
+            continue
+
+        def far_sends(group=group, which=which):
+            @pl.loop(0, half)
+            def _(step):
+                owner = lax.rem(inner + step, half)
+                for at in group[1:]:
+                    slot = slot_of(group, which, True, at, 1 - side)
+                    send(at, owner, slot, (1 - side) * half + owner, far_sem)
+
+        if which == 3:
+            pl.when(near)(far_sends)
+        else:
+            far_sends()
+
+        @pl.loop(1, half)
+        def _(step, group=group, which=which):
+            owner = lax.rem(inner + step, half)
             for at in group:
-                width = held[at].shape[2]
-                pltpu.make_async_remote_copy(
-                    src_ref=arrays[at].at[:, columns(width, peer)],
-                    dst_ref=held[at].at[me],
-                    send_sem=send_sem.at[at],
-                    recv_sem=recv_sem.at[at],
-                    device_id={"seq": peer},
-                    device_id_type=pl.DeviceIdType.MESH,
-                ).start()
+                slot = slot_of(group, which, True, at, side)
+                send(at, owner, slot, side * half + owner, send_sem)
 
     video_valid = video_length[0]
     audio_valid = audio_length[0]
     shift = align_offset[0]
-    video_total = n * held[0].shape[1]
-    audio_total = n * held[3].shape[1]
+    video_rows = arrays[0].shape[0]
+    audio_rows = arrays[3].shape[0]
+    video_total = n * video_rows
+    audio_total = n * audio_rows
     video_reach = video_total // 8
     audio_reach = 5 * audio_total // 8
 
-    def places(count, copies):
-        rows = lax.broadcasted_iota(jnp.int32, (count, 1), 0)
+    def query_places(count, copies, first):
+        rows = first + lax.broadcasted_iota(jnp.int32, (count, 1), 0)
         return jnp.concatenate([rows] * copies, axis=0)
 
     def key_places(count):
@@ -380,15 +446,16 @@
             return key_places(audio_total) < audio_valid
         if which == 2:
             where = key_places(audio_total)
-            spots = lax.shift_right_logical(places(video_total, copies), ratio.bit_length() - 1)
+            spots = query_places(half * video_rows, copies, side * half * video_rows)
+            spots = lax.shift_right_logical(spots, ratio.bit_length() - 1)
             center = jnp.clip(spots + shift, 0, audio_valid - 1)
             return (where < audio_valid) & (jnp.abs(where - center) <= audio_reach)
-        where = key_places(video_total)
-        spots = (places(audio_total, copies) - shift) * ratio
-        center = jnp.clip(spots, 0, video_valid - 1)
+        where = key_places((half + margin) * video_rows) + side * (half - margin) * video_rows
+        spots = query_places(half * audio_rows, copies, side * half * audio_rows)
+        center = jnp.clip((spots - shift) * ratio, 0, video_valid - 1)
         return (where < video_valid) & (jnp.abs(where - center) <= video_reach)
 
-    for group, which in zip(GROUPS, OUT_OF_GROUP):
+    for group, which, halved in GROUPS:
         for at in group:
             pltpu.make_async_copy(held[at], held[at], recv_sem.at[at]).wait()
         query, keys, values = (held[at] for at in group)
@@ -415,63 +482,103 @@
                     merged = jnp.where(lane == head, mixed[head * rows : (head + 1) * rows], merged)
                 mixed = merged
             write_tokens(results[which], column, mixed)
-        width = results[which].shape[2]
-        target = outs[which].at[:, columns(width, me)]
-        pltpu.make_async_copy(results[which].at[me], target, back_recv.at[which]).start()
-
-        @pl.loop(1, n)
-        def _(step, which=which, target=target):
-            peer = lax.rem(me + step, n)
+        mine = inner if halved else me
+        count = half if halved else n
+        first = side * half if halved else 0
+        target = outs[which].at[:, columns(results[which].shape[2], mine)]
+        pltpu.make_async_copy(results[which].at[mine], target, back_recv.at[which]).start()
+
+        @pl.loop(1, count)
+        def _(step, which=which, target=target, mine=mine, count=count, first=first):
+            block = lax.rem(mine + step, count)
             pltpu.make_async_remote_copy(
-                src_ref=results[which].at[peer],
+                src_ref=results[which].at[block],
                 dst_ref=target,
                 send_sem=back_send.at[which],
                 recv_sem=back_recv.at[which],
-                device_id={"seq": peer},
+                device_id={"seq": first + block},
                 device_id_type=pl.DeviceIdType.MESH,
             ).start()
 
-    for at in range(12):
-        part = held[at].at[pl.ds(0, n - 1)]
-        pltpu.make_async_copy(part, part, send_sem.at[at]).wait()
+    def wait_bytes(ref, blocks, sem):
+        part = ref.at[pl.ds(0, blocks)]
+        pltpu.make_async_copy(part, part, sem).wait()
+
+    for group, which, halved in GROUPS:
+        for at in group:
+            wait_bytes(held[at], half - 1, send_sem.at[at])
+            if not halved or (which == 2 and at != group[0]):
+                wait_bytes(held[at], half, far_sem.at[at])
+            elif at != group[0]:
+
+                @pl.when(near)
+                def _(at=at):
+                    wait_bytes(held[at], half, far_sem.at[at])
+
     for which in range(4):
-        part = results[which].at[pl.ds(0, n - 1)]
-        pltpu.make_async_copy(part, part, back_send.at[which]).wait()
+        wait_bytes(results[which], results[which].shape[0] - 1, back_send.at[which])
         pltpu.make_async_copy(outs[which], outs[which], back_recv.at[which]).wait()
+
+
+def write_out(*refs):
+    sources, targets, sem = refs[:4], refs[4:8], refs[8]
+    copies = [pltpu.make_async_copy(*pair, sem.at[at]) for at, pair in enumerate(zip(sources, targets))]
+    for copy in copies:
+        copy.start()
+    for copy in copies:
+        copy.wait()
 
 
 def fused_shards(*arguments):
     n = lax.axis_size("seq")
     arrays = arguments[:12]
     lengths = arguments[12:]
+    arrays = [pltpu.with_memory_space_constraint(a, pltpu.HBM) for a in arrays]
     ratio = arrays[0].shape[0] // arrays[3].shape[0]
-    held = [pltpu.VMEM((n, a.shape[0], a.shape[1] // n), a.dtype) for a in arrays]
-    results = [held[at] for at in (0, 3, 6, 9)]
-    outs = tuple(jax.ShapeDtypeStruct(arrays[at].shape, arrays[at].dtype) for at in (0, 3, 6, 9))
+    held = [pltpu.VMEM(s, a.dtype) for s, a in zip(held_shapes(n, arrays), arrays)]
+    results = [
+        pltpu.VMEM((n, *held[0].shape[1:]), jnp.bfloat16),
+        pltpu.VMEM((n, *held[3].shape[1:]), jnp.bfloat16),
+        pltpu.VMEM((n // 2, *held[6].shape[1:]), jnp.bfloat16),
+        pltpu.VMEM((n // 2, *held[9].shape[1:]), jnp.bfloat16),
+    ]
+    shapes = [arrays[at].shape for at in (0, 3, 6, 9)]
     anywhere = pl.BlockSpec(memory_space=pl.ANY)
     scalars = pl.BlockSpec(memory_space=pltpu.SMEM)
-    return pl.pallas_call(
+    vectors = pl.BlockSpec(memory_space=pltpu.VMEM)
+    mixed = pl.pallas_call(
         functools.partial(fused_kernel, n, ratio),
-        out_shape=outs,
-        in_specs=[scalars] * 3 + [anywhere] * 12,
-        out_specs=(anywhere,) * 4,
+        out_shape=tuple(pltpu.VMEM(shape, jnp.bfloat16) for shape in shapes),
+        in_specs=[scalars] * 3 + [pl.BlockSpec(memory_space=pltpu.HBM)] * 12,
+        out_specs=(vectors,) * 4,
         scratch_shapes=held
         + results
         + [
             pltpu.SemaphoreType.DMA((12,)),
             pltpu.SemaphoreType.DMA((12,)),
+            pltpu.SemaphoreType.DMA((12,)),
             pltpu.SemaphoreType.DMA((4,)),
             pltpu.SemaphoreType.DMA((4,)),
         ],
-        compiler_params=pltpu.CompilerParams(collective_id=0, has_side_effects=True),
+        compiler_params=pltpu.CompilerParams(
+            collective_id=0, has_side_effects=True, vmem_limit_bytes=24 * 2**20
+        ),
     )(*lengths, *arrays)
+    return pl.pallas_call(
+        write_out,
+        out_shape=tuple(jax.ShapeDtypeStruct(shape, jnp.bfloat16) for shape in shapes),
+        in_specs=[vectors] * 4,
+        out_specs=(anywhere,) * 4,
+        scratch_shapes=[pltpu.SemaphoreType.DMA((4,))],
+        compiler_params=pltpu.CompilerParams(vmem_limit_bytes=2**20),
+    )(*mixed)
 
 
 def kernel_fits(n, video_rows, audio_rows):
-    if n < 2 or HV % n or HA % n or (HV // n * HDV) % LANES or (HA // n * HDA) % LANES:
+    if n < 4 or n % 2 or HV % n or HA % n or (HV // n * HDV) % LANES or (HA // n * HDA) % LANES:
         return False
     ratio = video_rows // audio_rows
-    return video_rows == ratio * audio_rows and ratio & (ratio - 1) == 0 and audio_rows % 8 == 0
+    return video_rows == ratio * audio_rows and ratio & (ratio - 1) == 0 and n * audio_rows % 16 == 0 and audio_rows % 8 == 0
 
 
 def dispatch(*arguments):

time: 39.7 us -> 33.4 us (0.84)
  local copies, waits for them, and re-layouts: 3.8 us -> 0 us
  Pallas kernels: 33 us -> 30.6 us
    unnamed x10 -> x0, local copies, waits for them, and re-layouts: 3.8 us -> none
    pallas_call x1 -> x2, Pallas kernels: 33 us -> 30.6 us  [the longest x1 29.9 us: fused_shards(): pl.pallas_call(functools.partial(fused_kernel, n, ratio), out_shape=tuple...]
where the time goes in v2:
time: 33.4 us; the launch traced here: 33.2 us
  Pallas kernels  30.6 us (92%)
  between operations  2.58 us (8%)
    pallas_call x1, Pallas kernels, fused_shards(): pl.pallas_call(functools.partial(fused_kernel, n, ratio), out_shape=tuple...  29.9 us
    pallas_call x1, Pallas kernels, fused_shards(): pl.pallas_call(write_out, out_shape=tuple((jax.ShapeDtypeStruct(shape, jn...  0.73 us

profile of v2, /device:TPU:0, one launch (start us, length us, event | category | flops | bytes accessed | tf_op | source)
XLA Modules:
  0.0 33.2 jit_solution(8237154734729666405)
XLA Ops:
  2.6 29.9 %shard_map.174 = (bf16[16,4096]{1,0:T(8,128)(2,1)S(1)}, bf16[8,2048]{1,0:T(8,128)(2,1)S(1)}, bf16[16,2048]{1,0:T(8,128)(2,1)S(1)}, bf16[8,2048]{1,0:T(8,128)(2,1)S(1)}) custom-call(s32[1]{0:T(128)S(6)} %copy.19.refs_0_, s32[1]{0:T(128)S(6)} %copy.20.refs_1_, s32[1]{0:T(128)S(6)} %copy.21.refs_2_, bf16[16,4096]{1,0:T(8,128)(2,1)} %refs_3_.1, ...), custom_call_target="tpu_custom_call" | custom-call | tf_op jit(solution)/shard_map/pallas_call | solution.py:549
  32.5 0.7 %shard_map.175 = (bf16[16,4096]{1,0:T(8,128)(2,1)}, bf16[8,2048]{1,0:T(8,128)(2,1)}, bf16[16,2048]{1,0:T(8,128)(2,1)}, bf16[8,2048]{1,0:T(8,128)(2,1)}) custom-call(bf16[16,4096]{1,0:T(8,128)(2,1)S(1)} %get-tuple-element.8.refs_0_, bf16[8,2048]{1,0:T(8,128)(2,1)S(1)} %get-tuple-element.9.refs_1_, bf16[16,2048]{1,0:T(8,128)(2,1)S(1)} %get-tuple-element.10.refs_2_, ...), custom_call_target="tpu_custom_call" | custom-call | tf_op jit(solution)/shard_map/pallas_call | solution.py:567

commit v3 on v2

--- a/solution.py
+++ b/solution.py
@@ -281,8 +281,8 @@
 GROUPS = (
     ((0, 1, 2), 0, False),
     ((3, 4, 5), 1, False),
+    ((6, 10, 11), 2, True),
     ((9, 7, 8), 3, True),
-    ((6, 10, 11), 2, True),
 )
 
 

time: 33.4 us -> 33.1 us (level)
  no operation moved by 1% of the time
where the time goes in v3:
time: 33.1 us; the launch traced here: 32.9 us
  Pallas kernels  30.3 us (92%)
  between operations  2.58 us (8%)
    pallas_call x1, Pallas kernels, fused_shards(): pl.pallas_call(functools.partial(fused_kernel, n, ratio), out_shape=tuple...  29.6 us
    pallas_call x1, Pallas kernels, fused_shards(): pl.pallas_call(write_out, out_shape=tuple((jax.ShapeDtypeStruct(shape, jn...  0.73 us

profile of v3, /device:TPU:0, one launch (start us, length us, event | category | flops | bytes accessed | tf_op | source)
XLA Modules:
  0.0 32.9 jit_solution(12218664567584494750)
XLA Ops:
  2.6 29.6 %shard_map.174 = (bf16[16,4096]{1,0:T(8,128)(2,1)S(1)}, bf16[8,2048]{1,0:T(8,128)(2,1)S(1)}, bf16[16,2048]{1,0:T(8,128)(2,1)S(1)}, bf16[8,2048]{1,0:T(8,128)(2,1)S(1)}) custom-call(s32[1]{0:T(128)S(6)} %copy.19.refs_0_, s32[1]{0:T(128)S(6)} %copy.20.refs_1_, s32[1]{0:T(128)S(6)} %copy.21.refs_2_, bf16[16,4096]{1,0:T(8,128)(2,1)} %refs_3_.1, ...), custom_call_target="tpu_custom_call" | custom-call | tf_op jit(solution)/shard_map/pallas_call | solution.py:549
  32.2 0.7 %shard_map.175 = (bf16[16,4096]{1,0:T(8,128)(2,1)}, bf16[8,2048]{1,0:T(8,128)(2,1)}, bf16[16,2048]{1,0:T(8,128)(2,1)}, bf16[8,2048]{1,0:T(8,128)(2,1)}) custom-call(bf16[16,4096]{1,0:T(8,128)(2,1)S(1)} %get-tuple-element.8.refs_0_, bf16[8,2048]{1,0:T(8,128)(2,1)S(1)} %get-tuple-element.9.refs_1_, bf16[16,2048]{1,0:T(8,128)(2,1)S(1)} %get-tuple-element.10.refs_2_, ...), custom_call_target="tpu_custom_call" | custom-call | tf_op jit(solution)/shard_map/pallas_call | solution.py:567
